TPU v7x, 512 devices: a whole 4x4x16 slice. The times are simulated.
512 devices in a mesh: shell: 128 (over x, z, core), aux: 4 (over y).
Axes of the slice: x: 4, y: 4, z: 16, core: 2. Of those that a mesh axis runs over, the one named last changes fastest.
Arguments:
- integrals: bfloat16 [512, 128, 4, 128], P('shell', None, 'aux'), may hold values from -6 to 6
- pair_list: int32 [512, 3], P('shell'), may hold values from 0 to 511, as said below
- coef: bfloat16 [65536, 1024], P('shell'), may hold values from -0.5 to 0.5
- metric: bfloat16 [4, 4], replicated, may hold values from -3 to 3, as said below
- occ_slot: int32 [128], replicated, may hold values from 0 to 127, each once
Outputs:
- transformed: bfloat16 [1024, 4, 65536], P(('shell', 'aux'))
Inputs may be any that keep to these rules, and one draw needn't show every extreme that they name: `pair_list`: row d * 4 + k holds slot k of index d of shell: block row, block column, live flag. The block column lies in d * 4 to (d + 1) * 4 - 1. On every index live slots come first and at least one is live; some index has all 4 live. `metric`: lower triangular, positive on the diagonal.
All inputs are finite; a program needn't handle non-finite values.
Results may differ from a plain program's by a relative error of at most 0.0054.
Values may be sent and summed in bfloat16 or wider, within the bound.
A program may use at most 64 MiB of HBM per device.

v0:
```python
import jax
import jax.numpy as jnp
from jax import lax
from jax.sharding import PartitionSpec as P

BS = 128


def per_device(integrals, pair_list, coef, metric, occ_slot):
    pairs_dev = pair_list.shape[0]
    rows_local = coef.shape[0]
    occ_count = coef.shape[1]
    blocks_dev = rows_local // BS
    shell_count = lax.axis_size("shell")
    block_count = blocks_dev * shell_count
    slot_count = occ_slot.shape[0]
    aux_dev = integrals.shape[2]
    inverse = (
        jnp.zeros((slot_count,), jnp.int32)
        .at[occ_slot]
        .set(jnp.arange(slot_count, dtype=jnp.int32))
    )
    ordered = jnp.take(
        coef.reshape(rows_local, slot_count, occ_count // slot_count), inverse, axis=1
    )
    ordered = ordered.reshape(rows_local, occ_count)

    def one_slot(item):
        int_block, column_index = item
        start = column_index % blocks_dev * BS
        column = lax.dynamic_slice_in_dim(ordered, start, BS, 0)
        product = lax.dot_general(
            column,
            int_block.reshape(BS, aux_dev * BS),
            (((0,), (0,)), ((), ())),
            preferred_element_type=jnp.float32,
        )
        return product.astype(jnp.bfloat16)

    half_blocks = lax.map(one_slot, (integrals, pair_list[:, 1]))
    half_blocks = half_blocks.reshape(pairs_dev, occ_count, aux_dev, BS)
    listing = lax.all_gather(pair_list, "shell", axis=0, tiled=True)
    targets = jnp.arange(block_count, dtype=jnp.int32)[:, None]
    selector = ((listing[:, 0][None, :] == targets) & (listing[:, 2][None, :] == 1)).astype(
        jnp.bfloat16
    )
    relayed = lax.all_to_all(
        lax.all_to_all(half_blocks, "shell", split_axis=1, concat_axis=0, tiled=True),
        "aux",
        split_axis=1,
        concat_axis=2,
        tiled=True,
    )
    summed = jnp.dot(
        selector, relayed.reshape(relayed.shape[0], -1), preferred_element_type=jnp.float32
    )
    blocks = summed.astype(jnp.bfloat16).reshape((block_count,) + relayed.shape[1:])
    result = jnp.einsum("qp,bipm->iqbm", metric, blocks, preferred_element_type=jnp.float32)
    return result.reshape(result.shape[0], result.shape[1], block_count * BS).astype(jnp.bfloat16)


def solution(mesh):
    placed = (P("shell", None, "aux", None), P("shell", None), P("shell", None), P(), P())
    return jax.shard_map(
        per_device,
        mesh=mesh,
        in_specs=placed,
        out_specs=P(("shell", "aux"), None, None),
        check_vma=False,
    )
```

profile of v0, /device:TPU:1, one launch (start us, length us, event | category | flops | bytes accessed | tf_op | source)
XLA Modules:
  0.0 205.9 jit_solution(11804954031086884912)
XLA Ops:
  0.0 0.7 compare_select_fusion.1
  0.7 1.0 scatter_custom_fusion
  1.7 1.5 copy.23
  3.2 0.1 broadcast_in_dim.32
  3.3 0.1 broadcast_in_dim.33
  3.4 0.2 slice_reduce_fusion
  3.6 0.6 gather_fusion
  4.3 0.2 bitcast_select_fusion
  4.5 15.1 %while.12 = (s32[]{:T(128)}, bf16[4,1024,128]{2,1,0:T(8,128)(2,1)S(1)}, s32[4]{0:T(128)S(1)}, bf16[512,1024]{0,1:T(8,128)(2,1)S(1)}, bf16[4,128,1,128]{3,1,2,0:T...) while((s32[]{:T(128)}, ...), condition=%wide.region_2.3_spmd, body=%wide.region_1.2_spmd.sunk | while | flops 33685520 | bytes 558360 | solution.py:40
  4.5 0.7 dynamic_slice.31
  7.2 1.0 fusion.22
  8.3 0.7 dynamic_slice.31
  11.0 1.0 fusion.22
  12.0 0.7 dynamic_slice.31
  14.8 1.0 fusion.22
  15.8 0.7 dynamic_slice.31
  18.6 1.0 fusion.22
  19.6 0.8 copy.41
  20.4 74.5 %all_to_all.33 = bf16[4,1024,1,128]{3,0,2,1:T(4,128)(2,1)S(1)} all-to-all(bf16[4,1024,1,128]{3,0,2,1:T(4,128)(2,1)S(1)} %bitcast.50), channel_id=1, replica_groups=mesh['shell'=128,'aux'=4] {'shell'}, dimensions={1} | all-to-all | bytes 2097152 | tf_op jit(solution)/shard_map/all_to_all | solution.py:48
  94.9 0.1 copy.40
  95.1 0.2 copy.27
  95.3 1.1 copy.28
  96.4 4.2 %all-to-all-start.1 = ((bf16[512,8,1,128]{3,0,2,1:T(8,128)(2,1)}), bf16[512,8,1,128]{3,0,2,1:T(8,128)(2,1)S(1)}, u32[]{:S(2)}, u32[]{:S(2)}) async-start(bf16[512,8,1,128]{3,0,2,1:T(8,128)(2,1)} %copy.28), calls=%async_computation.1 | async-start | bytes 2097152 | tf_op jit(solution)/shard_map/all_to_all | solution.py:47
  100.6 100.8 %all-gather = s32[128,4,3]{2,1,0:T(4,128)S(1)} all-gather(s32[1,4,3]{2,1,0:T(4,128)S(1)} %bitcast.55), channel_id=1, replica_groups=mesh['shell'=128,'aux'=4] {'shell'}, dimensions={0}, use_global_device_ids=true | all-gather | bytes 6192 | tf_op jit(solution)/shard_map/all_gather | solution.py:42
  201.4 0.1 fusion.14
  201.5 0.1 copy.34
  201.7 0.1 copy.33
  201.8 0.5 copy.29
  202.4 0.7 convolution_convert_fusion.2
  203.1 0.8 reshape.43
  203.9 0.7 fusion.6
  204.6 1.3 copy.39
  (11 shorter events, 0.1 us)
Async XLA Ops:
  0.0 203.9 %copy-start = (bf16[4,4]{1,0:T(4,128)(2,1)S(1)}, bf16[4,4]{1,0:T(4,128)(2,1)}, u32[]{:S(2)}) copy-start(bf16[4,4]{1,0:T(4,128)(2,1)} %param.10) | copy-start | bytes 100
  1.7 1.7 copy-start.1
  96.4 105.4 %all-to-all-start.1 = ((bf16[512,8,1,128]{3,0,2,1:T(8,128)(2,1)}), bf16[512,8,1,128]{3,0,2,1:T(8,128)(2,1)S(1)}, u32[]{:S(2)}, u32[]{:S(2)}) async-start(bf16[512,8,1,128]{3,0,2,1:T(8,128)(2,1)} %copy.28), calls=%async_computation.1 | async-start | bytes 2097152 | tf_op jit(solution)/shard_map/all_to_all | solution.py:47
where the time goes:
time: 207 us; the launch traced here: 206 us
  blocking collectives  175 us (85%)
  local copies, waits for them, and re-layouts  11.4 us (6%)
  loops' own time  8.45 us (4%)
  matrix products  5.41 us (3%)
  starting transfers between devices  4.18 us (2%)
    all_gather x1, blocking collectives, per_device(): listing = lax.all_gather(pair_list, 'shell', axis=0, tiled=True)  101 us
    all_to_all x1, blocking collectives, per_device(): lax.all_to_all(half_blocks, 'shell', split_axis=1, concat_axis=0, tiled=T...  74.5 us
    another operation x1, loops' own time, per_device(): half_blocks = lax.map(one_slot, (integrals, pair_list[:, 1]))  8.45 us
    all_to_all x1, starting transfers between devices, per_device(): lax.all_to_all(lax.all_to_all(half_blocks, 'shell', split_axis=1, concat_...  4.18 us
  transfers between devices with their start and end apart: 1, of which 0 were waited for; matrix products, arithmetic and copies ran while one was open for 0% of the time, Pallas kernels for 0%

commit v1 on v0

--- a/solution.py
+++ b/solution.py
@@ -39,7 +39,8 @@
 
     half_blocks = lax.map(one_slot, (integrals, pair_list[:, 1]))
     half_blocks = half_blocks.reshape(pairs_dev, occ_count, aux_dev, BS)
-    listing = lax.all_gather(pair_list, "shell", axis=0, tiled=True)
+    outgoing = jnp.stack([pair_list] * lax.axis_size("shell"))
+    listing = jnp.concatenate(lax.all_to_all(outgoing, "shell", 0, 0), axis=0)
     targets = jnp.arange(block_count, dtype=jnp.int32)[:, None]
     selector = ((listing[:, 0][None, :] == targets) & (listing[:, 2][None, :] == 1)).astype(
         jnp.bfloat16

time: 207 us -> 150 us (0.72)
  blocking collectives: 175 us -> 0 us
  waiting for transfers between devices: 0.01 us -> 87.5 us
  starting transfers between devices: 4.18 us -> 33.1 us
    all_gather x1 -> x0, blocking collectives: 101 us -> none  [per_device(): listing = lax.all_gather(pair_list, 'shell', axis=0, tiled=True)]
    all_to_all x0 -> x2, waiting for transfers between devices: none -> 75.3 us  [the longest x1 54.3 us: per_device(): lax.all_to_all(half_blocks, 'shell', split_axis=1, concat_axis=0, tiled=T...]
    all_to_all x1 -> x0, blocking collectives: 74.5 us -> none  [per_device(): lax.all_to_all(half_blocks, 'shell', split_axis=1, concat_axis=0, tiled=T...]
    all_to_all x0 -> x2, starting transfers between devices: none -> 28.9 us  [the longest x1 20.4 us: per_device(): lax.all_to_all(half_blocks, 'shell', split_axis=1, concat_axis=0, tiled=T...]
    all_to_all x1, waiting for transfers between devices: 0.01 us -> 12.2 us  [per_device(): lax.all_to_all(lax.all_to_all(half_blocks, 'shell', split_axis=1, concat_...]
  transfers between devices with their start and end apart: 1 -> 3, of which waited for: 0 -> 3; matrix products, arithmetic and copies ran while one was open for 0% -> 1% of each run, Pallas kernels for 0% -> 0%
where the time goes in v1:
time: 150 us; the launch traced here: 148 us
  waiting for transfers between devices  87.5 us (58%)
  starting transfers between devices  33.1 us (22%)
  local copies, waits for them, and re-layouts  12.8 us (9%)
  loops' own time  7.78 us (5%)
  matrix products  5.42 us (4%)
    all_to_all x1, waiting for transfers between devices, per_device(): lax.all_to_all(half_blocks, 'shell', split_axis=1, concat_axis=0, tiled=T...  54.3 us
    all_to_all x1, waiting for transfers between devices, per_device(): listing = jnp.concatenate(lax.all_to_all(outgoing, 'shell', 0, 0), axis=0)  21 us
    all_to_all x1, starting transfers between devices, per_device(): lax.all_to_all(half_blocks, 'shell', split_axis=1, concat_axis=0, tiled=T...  20.4 us
    all_to_all x1, waiting for transfers between devices, per_device(): lax.all_to_all(lax.all_to_all(half_blocks, 'shell', split_axis=1, concat_...  12.2 us
    all_to_all x1, starting transfers between devices, per_device(): listing = jnp.concatenate(lax.all_to_all(outgoing, 'shell', 0, 0), axis=0)  8.48 us
    another operation x1, loops' own time, per_device(): half_blocks = lax.map(one_slot, (integrals, pair_list[:, 1]))  7.78 us
    all_to_all x1, starting transfers between devices, per_device(): lax.all_to_all(lax.all_to_all(half_blocks, 'shell', split_axis=1, concat_...  4.18 us
    dot_general x4, matrix products, one_slot(): lax.dot_general(column, int_block.reshape(BS, aux_dev * BS), (((0,), (0,)...  3.97 us
  transfers between devices with their start and end apart: 3, of which 3 were waited for; matrix products, arithmetic and copies ran while one was open for 1% of the time, Pallas kernels for 0%

profile of v1, /device:TPU:1, one launch (start us, length us, event | category | flops | bytes accessed | tf_op | source)
XLA Modules:
  0.0 147.7 jit_solution(13649713370472652099)
XLA Ops:
  0.0 0.7 compare_select_fusion.1
  0.7 1.0 scatter_custom_fusion
  1.7 1.5 %copy.21 = bf16[512,1024]{0,1:T(8,128)(2,1)S(1)} copy(bf16[512,1024]{1,0:T(8,128)(2,1)} %param.9) | data formatting | bytes 2097152 | tf_op args[2]
  3.4 0.2 slice_reduce_fusion
  3.6 0.6 gather_fusion
  4.3 0.2 bitcast_select_fusion
  4.5 14.2 %while.12 = (s32[]{:T(128)}, bf16[4,1024,128]{2,1,0:T(8,128)(2,1)S(1)}, s32[4]{0:T(128)S(1)}, bf16[512,1024]{0,1:T(8,128)(2,1)S(1)}, bf16[4,128,1,128]{3,1,2,0:T...) while((s32[]{:T(128)}, ...), condition=%wide.region_2.3_spmd, body=%wide.region_1.2_spmd.sunk | while | flops 33685520 | bytes 558360 | solution.py:40
  4.5 0.6 dynamic_slice.31
  7.0 1.0 fusion.21
  8.0 0.6 dynamic_slice.31
  10.6 1.0 fusion.21
  11.6 0.6 dynamic_slice.31
  14.1 1.0 fusion.21
  15.1 0.6 dynamic_slice.31
  17.7 1.0 fusion.21
  18.7 1.8 %copy.37 = bf16[4,1024,128]{2,0,1:T(4,128)(2,1)} copy(bf16[4,1024,128]{2,1,0:T(8,128)(2,1)S(1)} %get-tuple-element.71) | data formatting | bytes 2097152 | tf_op jit(solution)/shard_map/while | solution.py:40
  20.5 20.4 %all-to-all-start.1 = ((bf16[4,1024,1,128]{3,0,2,1:T(4,128)(2,1)}), bf16[4,1024,1,128]{3,0,2,1:T(4,128)(2,1)S(1)}, u32[]{:S(2)}, u32[]{:S(2)}) async-start(bf16[4,1024,1,128]{3,0,2,1:T(4,128)(2,1)} %bitcast.41), calls=%async_computation.1 | async-start | bytes 2097152 | tf_op jit(solution)/shard_map/all_to_all | solution.py:49
  41.0 54.3 %all-to-all-done.1 = bf16[4,1024,1,128]{3,0,2,1:T(4,128)(2,1)S(1)} async-done(((bf16[4,1024,1,128]{3,0,2,1:T(4,128)(2,1)}), bf16[4,1024,1,128]{3,0,2,1:T(4,128)(2,1)S(1)}, u32[]{:S(2)}, u32[]{:S(2)}) %all-to-all-start.1) | async-done | bytes 1048608 | tf_op jit(solution)/shard_map/all_to_all | solution.py:49
  95.2 0.7 stack.2
  95.9 8.5 %all-to-all-start = ((s32[128,4,3]{1,2,0:T(4,128)}), s32[128,4,3]{1,2,0:T(4,128)S(1)}, u32[]{:S(2)}, u32[]{:S(2)}) async-start(s32[128,4,3]{1,2,0:T(4,128)} %stack.2), calls=%async_computation | async-start | bytes 524288 | tf_op jit(solution)/shard_map/all_to_all | solution.py:43
  104.4 0.1 copy.36
  104.6 0.2 copy.25
  104.8 1.1 copy.26
  105.9 21.0 %all-to-all-done = s32[128,4,3]{1,2,0:T(4,128)S(1)} async-done(((s32[128,4,3]{1,2,0:T(4,128)}), s32[128,4,3]{1,2,0:T(4,128)S(1)}, u32[]{:S(2)}, u32[]{:S(2)}) %all-to-all-start) | async-done | bytes 6176 | tf_op jit(solution)/shard_map/all_to_all | solution.py:43
  126.9 4.2 %all-to-all-start.2 = ((bf16[512,8,1,128]{3,0,2,1:T(8,128)(2,1)}), bf16[512,8,1,128]{3,0,2,1:T(8,128)(2,1)S(1)}, u32[]{:S(2)}, u32[]{:S(2)}) async-start(bf16[512,8,1,128]{3,0,2,1:T(8,128)(2,1)} %copy.26), calls=%async_computation.2 | async-start | bytes 2097152 | tf_op jit(solution)/shard_map/all_to_all | solution.py:48
  131.1 0.1 reshape.45
  131.3 12.2 %all-to-all-done.2 = bf16[512,8,1,128]{3,0,2,1:T(8,128)(2,1)S(1)} async-done(((bf16[512,8,1,128]{3,0,2,1:T(8,128)(2,1)}), bf16[512,8,1,128]{3,0,2,1:T(8,128)(2,1)S(1)}, u32[]{:S(2)}, u32[]{:S(2)}) %all-to-all-start.2) | async-done | bytes 1048608 | tf_op jit(solution)/shard_map/all_to_all | solution.py:48
  143.6 0.5 copy.27
  144.1 0.8 convolution_convert_fusion.2
  144.8 0.8 reshape.49
  145.6 0.7 fusion.6
  146.3 1.3 copy.35
  (15 shorter events, 0.4 us)
Async XLA Ops:
  0.0 145.6 %copy-start = (bf16[4,4]{1,0:T(4,128)(2,1)S(1)}, bf16[4,4]{1,0:T(4,128)(2,1)}, u32[]{:S(2)}) copy-start(bf16[4,4]{1,0:T(4,128)(2,1)} %param.10) | copy-start | bytes 100
  1.7 1.7 %copy-start.1 = (s32[4,3]{1,0:T(4,128)S(1)}, s32[4,3]{1,0:T(4,128)}, u32[]{:S(2)}) copy-start(s32[4,3]{1,0:T(4,128)} %param.8) | copy-start | bytes 148
  20.5 74.8 %all-to-all-start.1 = ((bf16[4,1024,1,128]{3,0,2,1:T(4,128)(2,1)}), bf16[4,1024,1,128]{3,0,2,1:T(4,128)(2,1)S(1)}, u32[]{:S(2)}, u32[]{:S(2)}) async-start(bf16[4,1024,1,128]{3,0,2,1:T(4,128)(2,1)} %bitcast.41), calls=%async_computation.1 | async-start | bytes 2097152 | tf_op jit(solution)/shard_map/all_to_all | solution.py:49
  95.9 31.0 %all-to-all-start = ((s32[128,4,3]{1,2,0:T(4,128)}), s32[128,4,3]{1,2,0:T(4,128)S(1)}, u32[]{:S(2)}, u32[]{:S(2)}) async-start(s32[128,4,3]{1,2,0:T(4,128)} %stack.2), calls=%async_computation | async-start | bytes 524288 | tf_op jit(solution)/shard_map/all_to_all | solution.py:43
  126.9 16.6 %all-to-all-start.2 = ((bf16[512,8,1,128]{3,0,2,1:T(8,128)(2,1)}), bf16[512,8,1,128]{3,0,2,1:T(8,128)(2,1)S(1)}, u32[]{:S(2)}, u32[]{:S(2)}) async-start(bf16[512,8,1,128]{3,0,2,1:T(8,128)(2,1)} %copy.26), calls=%async_computation.2 | async-start | bytes 2097152 | tf_op jit(solution)/shard_map/all_to_all | solution.py:48
